TPU v7x, 32 devices: a whole 2x2x4 slice. The times are simulated.
32 devices in a mesh: fsdp: 8 (over y, x, core), tp: 4 (over z).
Axes of the slice: x: 2, y: 2, z: 4, core: 2. Of those that a mesh axis runs over, the one named last changes fastest.
Arguments:
- tokens: bfloat16 [16, 1376, 1024], P('fsdp', 'tp'), may hold values from -6 to 6
- w_query: bfloat16 [1024, 1024], P('fsdp', 'tp'), may hold values from -0.375 to 0.375
- w_key: bfloat16 [1024, 1024], P('fsdp', 'tp'), may hold values from -0.1875 to 0.1875
- w_value: bfloat16 [1024, 1024], P('fsdp', 'tp'), may hold values from -0.1875 to 0.1875
- w_out: bfloat16 [1024, 1024], P('tp', 'fsdp'), may hold values from -1 to 1
- w_up: bfloat16 [1024, 4096], P('fsdp', 'tp'), may hold values from -0.1875 to 0.1875
- w_down: bfloat16 [4096, 1024], P('tp', 'fsdp'), may hold values from -0.09375 to 0.09375
- norm1_gain: float32 [1024], replicated, may hold values from 0.5 to 1.5
- norm1_bias: float32 [1024], replicated, may hold values from -1.75 to 1.75
- query_bias: float32 [1024], replicated, may hold values from -3 to 3
- value_bias: float32 [1024], replicated, may hold values from -3 to 3
- out_bias: float32 [1024], replicated, may hold values from -1.75 to 1.75
- scale1: float32 [1024], replicated, may hold values from 0.5 to 1.5
- norm2_gain: float32 [1024], replicated, may hold values from 0.5 to 1.5
- norm2_bias: float32 [1024], replicated, may hold values from -1.75 to 1.75
- up_bias: float32 [4096], replicated, may hold values from -3 to 3
- down_bias: float32 [1024], replicated, may hold values from -1.75 to 1.75
- scale2: float32 [1024], replicated, may hold values from 0.5 to 1.5
- out_grad: bfloat16 [16, 1376, 1024], P('fsdp', 'tp'), may hold values from -6 to 6
Outputs:
- output: bfloat16 [16, 1376, 1024], P('fsdp', 'tp')
- tokens_grad: float32 [16, 1376, 1024], P('fsdp', 'tp')
- w_query_grad: float32 [1024, 1024], P('fsdp', 'tp')
- w_key_grad: float32 [1024, 1024], P('fsdp', 'tp')
- w_value_grad: float32 [1024, 1024], P('fsdp', 'tp')
- w_out_grad: float32 [1024, 1024], P('tp', 'fsdp')
- w_up_grad: float32 [1024, 4096], P('fsdp', 'tp')
- w_down_grad: float32 [4096, 1024], P('tp', 'fsdp')
- norm1_gain_grad: float32 [1024], replicated
- norm1_bias_grad: float32 [1024], replicated
- query_bias_grad: float32 [1024], replicated
- value_bias_grad: float32 [1024], replicated
- out_bias_grad: float32 [1024], replicated
- scale1_grad: float32 [1024], replicated
- norm2_gain_grad: float32 [1024], replicated
- norm2_bias_grad: float32 [1024], replicated
- up_bias_grad: float32 [4096], replicated
- down_bias_grad: float32 [1024], replicated
- scale2_grad: float32 [1024], replicated
All inputs are finite; a program needn't handle non-finite values.
Results may differ from a plain program's by a relative error of at most 0.02.
Values may be sent and summed in bfloat16 or wider, within the bound.
A program may use at most 256 MiB of HBM per device.

v0:
```python
import jax
import jax.numpy as jnp
from jax import lax
from jax.sharding import PartitionSpec as P

HD = 64
SEQ = 1370
Q_SPLIT = 2


norm_epsilon = 1e-06


def layer_norm(values, norm_gain, norm_bias):
    center = values - jnp.mean(values, axis=-1, keepdims=True)
    spread = jnp.mean(center * center, axis=-1, keepdims=True)
    return center * lax.rsqrt(spread + norm_epsilon) * norm_gain + norm_bias


def exact_gelu(values):
    return jax.nn.gelu(values, approximate=False)


def score_block(block_q, keys_all, key_valid):
    scores = (
        jnp.einsum("hqd,hkd->hqk", block_q, keys_all, preferred_element_type=jnp.float32) * 0.125
    )
    return jnp.where(key_valid, scores, -1e30)


def attend_image(queries, keys_all, values, key_valid):
    block_rows = queries.shape[1] // Q_SPLIT
    pieces = []
    log_pieces = []
    for block_index in range(Q_SPLIT):
        lower = block_index * block_rows
        scores = score_block(queries[:, lower : lower + block_rows], keys_all, key_valid)
        largest = jnp.max(scores, axis=-1, keepdims=True)
        expo = jnp.exp(scores - largest)
        totals = jnp.sum(expo, axis=-1, keepdims=True)
        shares = (expo / totals).astype(jnp.bfloat16)
        pieces.append(
            jnp.einsum("hqk,hkd->hqd", shares, values, preferred_element_type=jnp.float32)
        )
        log_pieces.append((largest + jnp.log(totals))[..., 0])
    return (
        jnp.concatenate(pieces, axis=1).astype(jnp.bfloat16),
        jnp.concatenate(log_pieces, axis=1),
    )


def attend_back(queries, keys_all, values, log_totals, grad_out, key_valid):
    block_rows = queries.shape[1] // Q_SPLIT
    grad_keys = jnp.zeros(keys_all.shape, jnp.float32)
    grad_values = jnp.zeros(values.shape, jnp.float32)
    query_pieces = []
    for block_index in range(Q_SPLIT):
        lower = block_index * block_rows
        block_q = queries[:, lower : lower + block_rows]
        block_grad = grad_out[:, lower : lower + block_rows]
        scores = score_block(block_q, keys_all, key_valid)
        shares = jnp.exp(scores - log_totals[:, lower : lower + block_rows, None])
        grad_values = grad_values + jnp.einsum(
            "hqk,hqd->hkd",
            shares.astype(jnp.bfloat16),
            block_grad,
            preferred_element_type=jnp.float32,
        )
        share_grad = jnp.einsum(
            "hqd,hkd->hqk", block_grad, values, preferred_element_type=jnp.float32
        )
        inner = jnp.sum(shares * share_grad, axis=-1, keepdims=True)
        score_grad = (shares * (share_grad - inner)).astype(jnp.bfloat16)
        query_pieces.append(
            jnp.einsum("hqk,hkd->hqd", score_grad, keys_all, preferred_element_type=jnp.float32)
            * 0.125
        )
        grad_keys = (
            grad_keys
            + jnp.einsum("hqk,hqd->hkd", score_grad, block_q, preferred_element_type=jnp.float32)
            * 0.125
        )
    return (jnp.concatenate(query_pieces, axis=1), grad_keys, grad_values)


def contract_rows(left, right):
    return lax.dot_general(
        left, right, (((0,), (0,)), ((), ())), preferred_element_type=jnp.float32
    )


def contract_cols(left, right):
    return lax.dot_general(
        left, right, (((1,), (1,)), ((), ())), preferred_element_type=jnp.float32
    )


def body(
    tokens,
    w_query,
    w_key,
    w_value,
    w_out,
    w_up,
    w_down,
    norm1_gain,
    norm1_bias,
    query_bias,
    value_bias,
    out_bias,
    scale1,
    norm2_gain,
    norm2_bias,
    up_bias,
    down_bias,
    scale2,
    out_grad,
):
    image_count, shard_rows, feature_width = tokens.shape
    tp_count = lax.axis_size("tp")
    tp_index = lax.axis_index("tp")
    local_rows = image_count * shard_rows
    seq_rows = shard_rows * tp_count
    flat_tokens = tokens.reshape(local_rows, feature_width)
    own_tokens = flat_tokens.astype(jnp.float32)
    group_tokens = lax.all_gather(flat_tokens, "tp", axis=0, tiled=True).astype(jnp.float32)
    gathered = (
        lax.all_gather(w_query, "fsdp", axis=0, tiled=True),
        lax.all_gather(w_key, "fsdp", axis=0, tiled=True),
        lax.all_gather(w_value, "fsdp", axis=0, tiled=True),
        lax.all_gather(w_out, "fsdp", axis=1, tiled=True),
        lax.all_gather(w_up, "fsdp", axis=0, tiled=True),
        lax.all_gather(w_down, "fsdp", axis=1, tiled=True),
    )
    head_cols = gathered[0].shape[1]
    hidden_cols = gathered[4].shape[1]
    heads_local = head_cols // HD
    query_slice = lax.dynamic_slice_in_dim(query_bias, tp_index * head_cols, head_cols)
    value_slice = lax.dynamic_slice_in_dim(value_bias, tp_index * head_cols, head_cols)
    up_slice = lax.dynamic_slice_in_dim(up_bias, tp_index * hidden_cols, hidden_cols)
    joint_bias = jnp.concatenate([query_slice, jnp.zeros((head_cols,), jnp.float32), value_slice])
    w_joint = jnp.concatenate([gathered[0], gathered[1], gathered[2]], axis=1)
    normed = layer_norm(group_tokens, norm1_gain, norm1_bias).astype(jnp.bfloat16)
    joint = (jnp.dot(normed, w_joint, preferred_element_type=jnp.float32) + joint_bias).astype(
        jnp.bfloat16
    )
    per_image = joint.reshape(tp_count, image_count, shard_rows, 3, heads_local, HD)
    per_image = per_image.transpose(1, 3, 4, 0, 2, 5).reshape(
        image_count, 3, heads_local, seq_rows, HD
    )
    key_valid = jnp.arange(seq_rows) < SEQ
    attended_list = []
    log_list = []
    for image_index in range(image_count):
        attended_one, log_one = attend_image(
            per_image[image_index, 0],
            per_image[image_index, 1],
            per_image[image_index, 2],
            key_valid,
        )
        attended_list.append(attended_one)
        log_list.append(log_one)
    attended_heads = jnp.stack(attended_list)
    attn_rows = attended_heads.reshape(image_count, heads_local, tp_count, shard_rows, HD)
    attn_rows = attn_rows.transpose(2, 0, 3, 1, 4).reshape(tp_count * local_rows, head_cols)
    w_proj = gathered[3]
    branch_own = (
        lax.psum_scatter(
            jnp.dot(attn_rows, w_proj, preferred_element_type=jnp.float32).astype(jnp.bfloat16),
            "tp",
            scatter_dimension=0,
            tiled=True,
        ).astype(jnp.float32)
        + out_bias
    )
    middle_own = own_tokens + scale1 * branch_own
    normed2_own = layer_norm(middle_own, norm2_gain, norm2_bias).astype(jnp.bfloat16)
    normed2 = lax.all_gather(normed2_own, "tp", axis=0, tiled=True)
    preact = jnp.dot(normed2, gathered[4], preferred_element_type=jnp.float32) + up_slice
    hidden = exact_gelu(preact).astype(jnp.bfloat16)
    w_second = gathered[5]
    feed_own = (
        lax.psum_scatter(
            jnp.dot(hidden, w_second, preferred_element_type=jnp.float32).astype(jnp.bfloat16),
            "tp",
            scatter_dimension=0,
            tiled=True,
        ).astype(jnp.float32)
        + down_bias
    )
    final = middle_own + scale2 * feed_own
    positions = tp_index * shard_rows + jnp.arange(shard_rows)
    row_valid = jnp.tile((positions < SEQ).astype(jnp.float32), image_count)[:, None]
    output = (
        (row_valid * final).astype(jnp.bfloat16).reshape(image_count, shard_rows, feature_width)
    )
    back_weights = (
        lax.all_gather(w_query, "fsdp", axis=0, tiled=True),
        lax.all_gather(w_key, "fsdp", axis=0, tiled=True),
        lax.all_gather(w_value, "fsdp", axis=0, tiled=True),
        lax.all_gather(w_out, "fsdp", axis=1, tiled=True),
        lax.all_gather(w_up, "fsdp", axis=0, tiled=True),
        lax.all_gather(w_down, "fsdp", axis=1, tiled=True),
    )
    back_joint = jnp.concatenate([back_weights[0], back_weights[1], back_weights[2]], axis=1)
    grad_final = row_valid * out_grad.reshape(local_rows, feature_width).astype(jnp.float32)
    scale2_grad = jnp.sum(grad_final * feed_own, axis=0)
    grad_feed = scale2 * grad_final
    down_bias_grad = jnp.sum(grad_feed, axis=0)
    feed_rows = lax.all_gather(grad_feed.astype(jnp.bfloat16), "tp", axis=0, tiled=True)
    w_down_part = contract_rows(hidden, feed_rows)
    hidden_grad = contract_cols(feed_rows, back_weights[5])
    gelu_value, gelu_back = jax.vjp(exact_gelu, preact)
    pre_grad = gelu_back(hidden_grad)[0]
    up_part = jnp.sum(pre_grad, axis=0)
    pre_low = pre_grad.astype(jnp.bfloat16)
    w_up_part = contract_rows(normed2, pre_low)
    w_first = back_weights[4]
    normed2_grad = lax.psum_scatter(
        contract_cols(pre_low, w_first).astype(jnp.bfloat16), "tp", scatter_dimension=0, tiled=True
    ).astype(jnp.float32)
    norm2_value, norm2_back = jax.vjp(layer_norm, middle_own, norm2_gain, norm2_bias)
    middle_part, norm2_gain_part, norm2_bias_part = norm2_back(normed2_grad)
    middle_grad = grad_final + middle_part
    scale1_part = jnp.sum(middle_grad * branch_own, axis=0)
    grad_branch = scale1 * middle_grad
    out_bias_part = jnp.sum(grad_branch, axis=0)
    branch_rows = lax.all_gather(grad_branch.astype(jnp.bfloat16), "tp", axis=0, tiled=True)
    w_out_part = contract_rows(attn_rows, branch_rows)
    attn_grad = contract_cols(branch_rows, back_weights[3]).astype(jnp.bfloat16)
    attn_grad = attn_grad.reshape(tp_count, image_count, shard_rows, heads_local, HD)
    attn_grad = attn_grad.transpose(1, 3, 0, 2, 4).reshape(image_count, heads_local, seq_rows, HD)
    grad_list = []
    for image_index in range(image_count):
        query_grad, key_grad, value_grad = attend_back(
            per_image[image_index, 0],
            per_image[image_index, 1],
            per_image[image_index, 2],
            log_list[image_index],
            attn_grad[image_index],
            key_valid,
        )
        grad_list.append(jnp.stack([query_grad, key_grad, value_grad]))
    joint_grad = jnp.stack(grad_list).reshape(image_count, 3, heads_local, tp_count, shard_rows, HD)
    joint_grad = joint_grad.transpose(3, 0, 4, 1, 2, 5).reshape(
        tp_count * local_rows, 3 * head_cols
    )
    query_part = jnp.sum(joint_grad[:, :head_cols], axis=0)
    value_part = jnp.sum(joint_grad[:, 2 * head_cols :], axis=0)
    joint_low = joint_grad.astype(jnp.bfloat16)
    w_joint_part = contract_rows(normed, joint_low)
    normed_grad = lax.psum_scatter(
        contract_cols(joint_low, back_joint).astype(jnp.bfloat16),
        "tp",
        scatter_dimension=0,
        tiled=True,
    ).astype(jnp.float32)
    norm1_value, norm1_back = jax.vjp(layer_norm, own_tokens, norm1_gain, norm1_bias)
    input_part, norm1_gain_part, norm1_bias_part = norm1_back(normed_grad)
    tokens_grad = (middle_grad + input_part).reshape(image_count, shard_rows, feature_width)
    weight_sums = (
        lax.psum_scatter(
            w_joint_part[:, :head_cols].astype(jnp.bfloat16),
            "fsdp",
            scatter_dimension=0,
            tiled=True,
        ).astype(jnp.float32),
        lax.psum_scatter(
            w_joint_part[:, head_cols : 2 * head_cols].astype(jnp.bfloat16),
            "fsdp",
            scatter_dimension=0,
            tiled=True,
        ).astype(jnp.float32),
        lax.psum_scatter(
            w_joint_part[:, 2 * head_cols :].astype(jnp.bfloat16),
            "fsdp",
            scatter_dimension=0,
            tiled=True,
        ).astype(jnp.float32),
        lax.psum_scatter(
            w_out_part.astype(jnp.bfloat16), "fsdp", scatter_dimension=1, tiled=True
        ).astype(jnp.float32),
        lax.psum_scatter(
            w_up_part.astype(jnp.bfloat16), "fsdp", scatter_dimension=0, tiled=True
        ).astype(jnp.float32),
        lax.psum_scatter(
            w_down_part.astype(jnp.bfloat16), "fsdp", scatter_dimension=1, tiled=True
        ).astype(jnp.float32),
    )
    query_full = lax.dynamic_update_slice_in_dim(
        jnp.zeros_like(query_bias), query_part, tp_index * head_cols, 0
    )
    value_full = lax.dynamic_update_slice_in_dim(
        jnp.zeros_like(value_bias), value_part, tp_index * head_cols, 0
    )
    up_full = lax.dynamic_update_slice_in_dim(
        jnp.zeros_like(up_bias), up_part, tp_index * hidden_cols, 0
    )
    small_sums = lax.psum(
        (
            norm1_gain_part,
            norm1_bias_part,
            query_full,
            value_full,
            out_bias_part,
            scale1_part,
            norm2_gain_part,
            norm2_bias_part,
            up_full,
            down_bias_grad,
            scale2_grad,
        ),
        ("fsdp", "tp"),
    )
    return (
        output,
        tokens_grad,
        weight_sums[0],
        weight_sums[1],
        weight_sums[2],
        weight_sums[3],
        weight_sums[4],
        weight_sums[5],
        small_sums[0],
        small_sums[1],
        small_sums[2],
        small_sums[3],
        small_sums[4],
        small_sums[5],
        small_sums[6],
        small_sums[7],
        small_sums[8],
        small_sums[9],
        small_sums[10],
    )


def solution(mesh):
    placed = (
        P("fsdp", "tp", None),
        P("fsdp", "tp"),
        P("fsdp", "tp"),
        P("fsdp", "tp"),
        P("tp", "fsdp"),
        P("fsdp", "tp"),
        P("tp", "fsdp"),
        P(),
        P(),
        P(),
        P(),
        P(),
        P(),
        P(),
        P(),
        P(),
        P(),
        P(),
        P("fsdp", "tp", None),
    )
    return jax.shard_map(
        body,
        mesh=mesh,
        in_specs=placed,
        out_specs=(
            P("fsdp", "tp", None),
            P("fsdp", "tp", None),
            P("fsdp", "tp"),
            P("fsdp", "tp"),
            P("fsdp", "tp"),
            P("tp", "fsdp"),
            P("fsdp", "tp"),
            P("tp", "fsdp"),
            P(),
            P(),
            P(),
            P(),
            P(),
            P(),
            P(),
            P(),
            P(),
            P(),
            P(),
        ),
        check_vma=False,
    )
```

profile of v0, /device:TPU:0, one launch (start us, length us, event | category | flops | bytes accessed | tf_op | source)
XLA Modules:
  0.0 1545.7 jit_solution(12800401797097320902)
XLA Ops:
  10.4 13.4 all_gather.40
  23.8 9.2 all_gather.37
  32.9 9.5 all_gather.38
  42.4 9.2 all_gather.39
  51.8 65.9 %all-gather.7.cloned.1.call-done = bf16[2752,1024]{1,0:T(8,128)(2,1)} async-done(((bf16[688,1024]{1,0:T(8,128)(2,1)}), bf16[2752,1024]{1,0:T(8,128)(2,1)}) %all-gather.7.cloned.1.call-update) | async-done | bytes 5636112 | tf_op jit(solution)/shard_map/all_gather | solution.py:126
  138.0 10.0 reshape.282
  155.0 9.1 reshape.283
  165.7 9.7 fusion.109
  175.4 7.8 fusion.110
  183.3 8.0 fusion.107
  191.3 7.8 fusion.108
  199.1 8.0 fusion.1
  245.5 7.6 fusion.2
  282.4 97.9 %reduce-scatter.15.cloned.1.call-done = bf16[688,1024]{1,0:T(8,128)(2,1)} async-done(((bf16[2752,1024]{1,0:T(8,128)(2,1)}), bf16[688,1024]{1,0:T(8,128)(2,1)}) %reduce-scatter.15.cloned.1.call-update) | async-done | bytes 1409040 | tf_op jit(solution)/shard_map/reduce_scatter | solution.py:168
  391.5 99.7 %all-gather.9.cloned.1.call-done = bf16[2752,1024]{1,0:T(8,128)(2,1)} async-done(((bf16[688,1024]{1,0:T(8,128)(2,1)}), bf16[2752,1024]{1,0:T(8,128)(2,1)}) %all-gather.9.cloned.1.call-update) | async-done | bytes 5636112 | tf_op jit(solution)/shard_map/all_gather | solution.py:178
  491.2 11.1 fusion.111
  502.4 16.9 %all-gather.13.cloned.1.call-done = bf16[1024,1024]{1,0:T(8,128)(2,1)} async-done(((bf16[1024,128]{1,0:T(8,128)(2,1)}), bf16[1024,1024]{1,0:T(8,128)(2,1)}) %all-gather.13.cloned.1.call-update) | async-done | bytes 2097168 | tf_op jit(solution)/shard_map/all_gather | solution.py:133
  519.2 106.6 %all-gather.15.cloned.1.call-done = bf16[2752,1024]{1,0:T(8,128)(2,1)} async-done(((bf16[688,1024]{1,0:T(8,128)(2,1)}), bf16[2752,1024]{1,0:T(8,128)(2,1)}) %all-gather.15.cloned.1.call-update) | async-done | bytes 5636112 | tf_op jit(solution)/shard_map/all_gather | solution.py:210
  625.8 36.6 %fusion.104 = (f32[1024]{0:T(1024)}, bf16[2752,1024]{1,0:T(8,128)(2,1)S(1)}, f32[2752,1024]{1,0:T(8,128)}) fusion(f32[2752,1024]{1,0:T(8,128)} %fusion.111, f32[1024]{0:T(1024)S(1)} %dynamic_slice.11, bf16[2752,1024]{1,0:T(8,128)(2,1)} %all-gather.15.cloned.1.call-done, bf16[1024,1024]{1,0:T(8,128)(2,1)} %all-gather.13.cloned.1.call-done), kind=kOutput, calls=%fused_computation.203 | convolution fusion | flops 5979896832 | bytes 35921920 | tf_op jit(solution)/shard_map/dot_general | solution.py:93
  664.8 8.1 convolution_convert_fusion.2
  673.2 9.8 multiply_convert_fusion.4
  685.4 7.8 convolution_convert_fusion.3
  693.3 78.2 %reduce-scatter.19.cloned.1.call-done = bf16[688,1024]{1,0:T(8,128)(2,1)} async-done(((bf16[2752,1024]{1,0:T(8,128)(2,1)}), bf16[688,1024]{1,0:T(8,128)(2,1)}) %reduce-scatter.19.cloned.1.call-update) | async-done | bytes 1409040 | tf_op jit(solution)/shard_map/reduce_scatter | solution.py:219
  777.8 96.6 %reduce-scatter.17.cloned.1.call-done = bf16[688,1024]{1,0:T(8,128)(2,1)} async-done(((bf16[2752,1024]{1,0:T(8,128)(2,1)}), bf16[688,1024]{1,0:T(8,128)(2,1)}) %reduce-scatter.17.cloned.1.call-update) | async-done | bytes 1409040 | tf_op jit(solution)/shard_map/reduce_scatter | solution.py:183
  883.5 9.9 convolution_convert_fusion.5
  896.4 10.9 fusion.62
  907.7 80.8 %all-gather.17.cloned.1.call-done = bf16[2752,1024]{1,0:T(8,128)(2,1)} async-done(((bf16[688,1024]{1,0:T(8,128)(2,1)}), bf16[2752,1024]{1,0:T(8,128)(2,1)}) %all-gather.17.cloned.1.call-update) | async-done | bytes 5636112 | tf_op jit(solution)/shard_map/all_gather | solution.py:228
  997.9 10.5 slice_reduce_fusion.3
  1008.9 9.6 fusion.20
  1018.6 12.1 multiply_reduce_fusion
  1030.7 9.2 multiply_reduce_fusion.1
  1039.9 10.0 multiply_convert_fusion.1
  1061.1 9.3 fusion.24
  1070.5 12.0 multiply_reduce_fusion.2
  1082.5 8.8 multiply_reduce_fusion.3
  1091.3 9.8 multiply_convert_fusion.3
  1113.7 9.2 fusion.56
  1126.8 14.8 multiply_convert_fusion
  1154.1 10.0 multiply_convert_fusion.2
  1213.3 12.6 maximum_bitcast_fusion
  1225.9 14.4 reshape.287
  1240.7 11.1 fusion.66
  1254.4 10.1 convolution_convert_fusion
  1276.7 33.3 %reduce-scatter.23.cloned.1.call-done = bf16[128,256]{1,0:T(8,128)(2,1)} async-done(((bf16[1024,256]{1,0:T(8,128)(2,1)}), bf16[128,256]{1,0:T(8,128)(2,1)}) %reduce-scatter.23.cloned.1.call-update) | async-done | bytes 65552 | tf_op jit(solution)/shard_map/reduce_scatter | solution.py:262
  1311.5 35.7 %reduce-scatter.25.cloned.1.call-done = bf16[128,256]{1,0:T(8,128)(2,1)} async-done(((bf16[1024,256]{1,0:T(8,128)(2,1)}), bf16[128,256]{1,0:T(8,128)(2,1)}) %reduce-scatter.25.cloned.1.call-update) | async-done | bytes 65552 | tf_op jit(solution)/shard_map/reduce_scatter | solution.py:268
  1348.7 35.6 %reduce-scatter.27.cloned.1.call-done = bf16[128,256]{1,0:T(8,128)(2,1)} async-done(((bf16[1024,256]{1,0:T(8,128)(2,1)}), bf16[128,256]{1,0:T(8,128)(2,1)}) %reduce-scatter.27.cloned.1.call-update) | async-done | bytes 65552 | tf_op jit(solution)/shard_map/reduce_scatter | solution.py:274
  1385.7 101.0 %reduce-scatter.21.cloned.1.call-done = bf16[688,1024]{1,0:T(8,128)(2,1)} async-done(((bf16[2752,1024]{1,0:T(8,128)(2,1)}), bf16[688,1024]{1,0:T(8,128)(2,1)}) %reduce-scatter.21.cloned.1.call-update) | async-done | bytes 1409040 | tf_op jit(solution)/shard_map/reduce_scatter | solution.py:252
  1492.1 42.4 %all-reduce = (f32[1024]{0:T(1024)}, f32[1024]{0:T(1024)}, f32[1024]{0:T(1024)}, f32[1024]{0:T(1024)}, f32[1024]{0:T(1024)}, /*index=5*/f32[1024]{0:T(1024)}, f3...) all-reduce(f32[1024]{0:T(1024)S(1)} %get-tuple-element.27, ...), channel_id=1, replica_groups=mesh['fsdp'=8,'tp'=4] {'fsdp','tp'}, use_global_device_ids=true, to_apply=%region_33.34 | all-reduce | flops 14336 | bytes 114688 | tf_op jit(solution)/shard_map/psum | solution.py:299
  (315 shorter events, 260.8 us)
Async XLA Ops:
  8.0 109.7 %all-gather.7.cloned.1.call-start = ((), (), s32[]{:S(2)}) async-start(), calls=%async_computation.10 | async-start | bytes 7045120 | tf_op jit(solution)/shard_map/all_gather | solution.py:126
  8.8 371.6 %reduce-scatter.15.cloned.1.call-start = ((), (), s32[]{:S(2)}) async-start(), calls=%async_computation.11 | async-start | bytes 7045120 | tf_op jit(solution)/shard_map/reduce_scatter | solution.py:168
  51.7 71.8 %copy-start.19 = (bf16[1024,768]{1,0:T(8,128)(2,1)}, bf16[1024,768]{1,0:T(8,128)(2,1)S(1)}, u32[]{:S(2)}) copy-start(bf16[1024,768]{1,0:T(8,128)(2,1)S(1)} %constant_dynamic-update-slice_fusion) | copy-start | bytes 4718596
  51.7 72.5 %copy-start.51 = (f32[1024]{0:T(1024)S(1)}, f32[1024]{0:T(1024)}, u32[]{:S(2)}) copy-start(f32[1024]{0:T(1024)} %param.26) | copy-start | bytes 12292
  51.8 72.4 %copy-start.69 = (f32[1024]{0:T(1024)S(1)}, f32[1024]{0:T(1024)}, u32[]{:S(2)}) copy-start(f32[1024]{0:T(1024)} %param.27) | copy-start | bytes 12292
  165.7 25.6 %copy-start.8 = (bf16[4,1376,64]{1,2,0:T(8,128)(2,1)}, bf16[4,1376,64]{1,2,0:T(8,128)(2,1)S(1)}, u32[]{:S(2)}) copy-start(bf16[4,1376,64]{1,2,0:T(8,128)(2,1)S(1)} %get-tuple-element.49) | copy-start | bytes 2113540
  175.4 31.8 %copy-start.21 = (f32[4,688]{1,0:T(4,128)}, f32[4,688]{1,0:T(4,128)S(1)}, u32[]{:S(2)}) copy-start(f32[4,688]{1,0:T(4,128)S(1)} %get-tuple-element.61) | copy-start | bytes 33028
  183.3 38.6 %copy-start.23 = (f32[4,688]{1,0:T(4,128)}, f32[4,688]{1,0:T(4,128)S(1)}, u32[]{:S(2)}) copy-start(f32[4,688]{1,0:T(4,128)S(1)} %get-tuple-element.63) | copy-start | bytes 33028
  191.3 46.6 %copy-start.25 = (f32[4,688]{1,0:T(4,128)}, f32[4,688]{1,0:T(4,128)S(1)}, u32[]{:S(2)}) copy-start(f32[4,688]{1,0:T(4,128)S(1)} %get-tuple-element.57) | copy-start | bytes 33028
  199.1 54.0 %copy-start.27 = (f32[4,688]{1,0:T(4,128)}, f32[4,688]{1,0:T(4,128)S(1)}, u32[]{:S(2)}) copy-start(f32[4,688]{1,0:T(4,128)S(1)} %get-tuple-element.59) | copy-start | bytes 33028
  281.7 98.6 %copy-start.49 = (f32[1024]{0:T(1024)S(1)}, f32[1024]{0:T(1024)}, u32[]{:S(2)}) copy-start(f32[1024]{0:T(1024)} %param.31) | copy-start | bytes 12292
  281.7 98.6 %copy-start.58 = (f32[1024]{0:T(1024)S(1)}, f32[1024]{0:T(1024)}, u32[]{:S(2)}) copy-start(f32[1024]{0:T(1024)} %param.30) | copy-start | bytes 12292
  281.7 109.8 %all-gather.11.cloned.1.call-start = ((), (), s32[]{:S(2)}) async-start(), calls=%async_computation.13 | async-start | bytes 2359296 | tf_op jit(solution)/shard_map/all_gather | solution.py:132
  282.3 102.2 %copy-start.31 = (f32[1024]{0:T(1024)S(1)}, f32[1024]{0:T(1024)}, u32[]{:S(2)}) copy-start(f32[1024]{0:T(1024)} %param.32) | copy-start | bytes 12292
  282.3 102.2 %copy-start.66 = (f32[1024]{0:T(1024)S(1)}, f32[1024]{0:T(1024)}, u32[]{:S(2)}) copy-start(f32[1024]{0:T(1024)} %param.33) | copy-start | bytes 12292
  282.3 208.9 %all-gather.9.cloned.1.call-start = ((), (), s32[]{:S(2)}) async-start(), calls=%async_computation.12 | async-start | bytes 7045120 | tf_op jit(solution)/shard_map/all_gather | solution.py:178
  386.2 133.1 %all-gather.13.cloned.1.call-start = ((), (), s32[]{:S(2)}) async-start(), calls=%async_computation.14 | async-start | bytes 2359296 | tf_op jit(solution)/shard_map/all_gather | solution.py:133
  386.8 239.1 %all-gather.15.cloned.1.call-start = ((), (), s32[]{:S(2)}) async-start(), calls=%async_computation.16 | async-start | bytes 7045120 | tf_op jit(solution)/shard_map/all_gather | solution.py:210
  387.9 114.5 %copy-start.45 = (f32[688]{0:T(1024)}, f32[688]{0:T(1024)S(1)}, u32[]{:S(2)}) copy-start(f32[688]{0:T(1024)S(1)} %mul.291) | copy-start | bytes 8260
  390.8 380.8 %reduce-scatter.19.cloned.1.call-start = ((), (), s32[]{:S(2)}) async-start(), calls=%async_computation.17 | async-start | bytes 7045120 | tf_op jit(solution)/shard_map/reduce_scatter | solution.py:219
  625.8 39.0 %copy-start.67 = (bf16[1024,1024]{1,0:T(8,128)(2,1)S(1)}, bf16[1024,1024]{1,0:T(8,128)(2,1)}, u32[]{:S(2)}) copy-start(bf16[1024,1024]{1,0:T(8,128)(2,1)} %all-gather.11.cloned.1.call-done) | copy-start | bytes 6291460
  673.0 201.5 %reduce-scatter.17.cloned.1.call-start = ((), (), s32[]{:S(2)}) async-start(), calls=%async_computation.15 | async-start | bytes 7045120 | tf_op jit(solution)/shard_map/reduce_scatter | solution.py:183
  693.2 81.2 %copy-start.48 = (f32[688]{0:T(1024)S(1)}, f32[688]{0:T(1024)}, u32[]{:S(2)}) copy-start(f32[688]{0:T(1024)} %copy-done.47) | copy-start | bytes 8260
  693.2 81.2 %copy-start.30 = (f32[688]{0:T(1024)S(1)}, f32[688]{0:T(1024)}, u32[]{:S(2)}) copy-start(f32[688]{0:T(1024)} %copy-done.29) | copy-start | bytes 8260
  693.2 181.2 %copy-start.43 = (f32[1024]{0:T(1024)S(1)}, f32[1024]{0:T(1024)}, u32[]{:S(2)}) copy-start(f32[1024]{0:T(1024)} %param.36) | copy-start | bytes 12292
  693.2 181.2 %copy-start.46 = (f32[688]{0:T(1024)S(1)}, f32[688]{0:T(1024)}, u32[]{:S(2)}) copy-start(f32[688]{0:T(1024)} %copy-done.45) | copy-start | bytes 8260
  693.2 181.2 %copy-start.50 = (f32[1024]{0:T(1024)S(1)}, f32[1024]{0:T(1024)}, u32[]{:S(2)}) copy-start(f32[1024]{0:T(1024)} %param.31) | copy-start | bytes 12292
  693.2 181.2 %copy-start.59 = (f32[1024]{0:T(1024)S(1)}, f32[1024]{0:T(1024)}, u32[]{:S(2)}) copy-start(f32[1024]{0:T(1024)} %param.30) | copy-start | bytes 12292
  693.3 181.2 %copy-start.64 = (f32[1024]{0:T(1024)S(1)}, f32[1024]{0:T(1024)}, u32[]{:S(2)}) copy-start(f32[1024]{0:T(1024)} %param.35) | copy-start | bytes 12292
  693.3 295.2 %all-gather.17.cloned.1.call-start = ((), (), s32[]{:S(2)}) async-start(), calls=%async_computation.18 | async-start | bytes 7045120 | tf_op jit(solution)/shard_map/all_gather | solution.py:228
  883.5 384.2 %reduce-scatter.33.cloned.1.call-start = ((), (), s32[]{:S(2)}) async-start(), calls=%async_computation.25 | async-start | bytes 2359296
  896.1 373.5 %reduce-scatter.29.cloned.1.call-start = ((), (), s32[]{:S(2)}) async-start(), calls=%async_computation.23 | async-start | bytes 2359296 | tf_op jit(solution)/shard_map/reduce_scatter | solution.py:283
  896.4 92.2 %copy-start.16 = (bf16[256,1024]{1,0:T(8,128)(2,1)S(1)}, bf16[256,1024]{1,0:T(8,128)(2,1)}, u32[]{:S(2)}) copy-start(bf16[256,1024]{1,0:T(8,128)(2,1)} %all_gather.40) | copy-start | bytes 1572868
  907.3 367.8 %reduce-scatter.31.cloned.1.call-start = ((), (), s32[]{:S(2)}) async-start(), calls=%async_computation.24 | async-start | bytes 589824
  1008.9 21.7 %slice-start.8 = ((s8[15499264]{0:T(1024)(128)(4,1)}), s8[4194304]{0:T(1024)(128)(4,1)S(1)}, s32[]{:S(2)}) async-start(s8[15499264]{0:T(1024)(128)(4,1)} %bitcast.143), calls=%async_computation.34 | async-start | bytes 8388608
  1126.8 27.3 %slice-start = ((s8[15499264]{0:T(1024)(128)(4,1)}), s8[4194304]{0:T(1024)(128)(4,1)S(1)}, s32[]{:S(2)}) async-start(s8[15499264]{0:T(1024)(128)(4,1)} %bitcast.139), calls=%async_computation.26 | async-start | bytes 8388608
  1126.8 27.3 %slice-start.1 = ((s8[15499264]{0:T(1024)(128)(4,1)}), s8[4194304]{0:T(1024)(128)(4,1)S(1)}, s32[]{:S(2)}) async-start(s8[15499264]{0:T(1024)(128)(4,1)} %bitcast.139), calls=%async_computation.27 | async-start | bytes 8388608
  1126.8 27.3 %slice-start.2 = ((s8[15499264]{0:T(1024)(128)(4,1)}), s8[4194304]{0:T(1024)(128)(4,1)S(1)}, s32[]{:S(2)}) async-start(s8[15499264]{0:T(1024)(128)(4,1)} %bitcast.139), calls=%async_computation.28 | async-start | bytes 8388608
  1240.4 69.6 %reduce-scatter.23.cloned.1.call-start = ((), (), s32[]{:S(2)}) async-start(), calls=%async_computation.20 | async-start | bytes 589824 | tf_op jit(solution)/shard_map/reduce_scatter | solution.py:262
  1253.0 94.1 %reduce-scatter.25.cloned.1.call-start = ((), (), s32[]{:S(2)}) async-start(), calls=%async_computation.21 | async-start | bytes 589824 | tf_op jit(solution)/shard_map/reduce_scatter | solution.py:268
  1253.8 130.4 %reduce-scatter.27.cloned.1.call-start = ((), (), s32[]{:S(2)}) async-start(), calls=%async_computation.22 | async-start | bytes 589824 | tf_op jit(solution)/shard_map/reduce_scatter | solution.py:274
  1254.4 232.3 %reduce-scatter.21.cloned.1.call-start = ((), (), s32[]{:S(2)}) async-start(), calls=%async_computation.19 | async-start | bytes 7045120 | tf_op jit(solution)/shard_map/reduce_scatter | solution.py:252
  1271.4 220.6 %copy-start.55 = (f32[1024]{0:T(1024)S(1)}, f32[1024]{0:T(1024)}, u32[]{:S(2)}) copy-start(f32[1024]{0:T(1024)} %get-tuple-element.23) | copy-start | bytes 12292
  1271.4 220.6 %copy-start.56 = (f32[1024]{0:T(1024)S(1)}, f32[1024]{0:T(1024)}, u32[]{:S(2)}) copy-start(f32[1024]{0:T(1024)} %get-tuple-element.24) | copy-start | bytes 12292
  1271.4 220.7 %copy-start.57 = (f32[1024]{0:T(1024)S(1)}, f32[1024]{0:T(1024)}, u32[]{:S(2)}) copy-start(f32[1024]{0:T(1024)} %get-tuple-element.51) | copy-start | bytes 12292
  1271.4 220.7 %copy-start.60 = (f32[1024]{0:T(1024)S(1)}, f32[1024]{0:T(1024)}, u32[]{:S(2)}) copy-start(f32[1024]{0:T(1024)} %get-tuple-element.29) | copy-start | bytes 12292
  1271.4 220.7 %copy-start.61 = (f32[1024]{0:T(1024)S(1)}, f32[1024]{0:T(1024)}, u32[]{:S(2)}) copy-start(f32[1024]{0:T(1024)} %get-tuple-element.21) | copy-start | bytes 12292
  1486.7 47.8 %copy-start.5 = (bf16[688,1024]{1,0:T(8,128)(2,1)S(1)}, bf16[688,1024]{1,0:T(8,128)(2,1)}, u32[]{:S(2)}) copy-start(bf16[688,1024]{1,0:T(8,128)(2,1)} %reduce-scatter.21.cloned.1.call-done) | copy-start | bytes 4227076
  (54 other events, 388.7 us)
Sparse Core Ops, SparseCore 0:
  10.4 107.2 all-gather.6
  281.8 98.4 reduce-scatter.14
  673.1 98.4 reduce-scatter.18
  773.7 100.6 reduce-scatter.16
Sparse Core Ops, SparseCore 1:
  284.1 25.9 all-gather.10
  386.3 104.9 all-gather.8
  493.0 26.2 all-gather.12
  521.4 104.4 all-gather.14
  883.6 104.9 all-gather.16
  991.8 39.2 reduce-scatter.32
  1034.2 41.0 reduce-scatter.28
  1240.4 32.4 reduce-scatter.30
  1275.8 34.1 reduce-scatter.22
  1313.1 34.0 reduce-scatter.24
  1350.1 34.1 reduce-scatter.26
  1386.6 100.1 reduce-scatter.20
where the time goes:
time: 1560 us; the launch traced here: 1550 us
  waiting for transfers between devices  851 us (55%)
  matrix products  311 us (20%)
  other arithmetic  155 us (10%)
  local copies, waits for them, and re-layouts  126 us (8%)
  blocking collectives  83.6 us (5%)
  between operations  17 us (1%)
    all_gather x1, waiting for transfers between devices, body(): lax.all_gather(grad_feed.astype(jnp.bfloat16), 'tp', axis=0, tiled=True)  107 us
    reduce_scatter x1, waiting for transfers between devices, body(): lax.psum_scatter(contract_cols(joint_low, back_joint).astype(jnp.bfloat16...  101 us
    all_gather x1, waiting for transfers between devices, body(): normed2 = lax.all_gather(normed2_own, 'tp', axis=0, tiled=True)  99.7 us
    reduce_scatter x1, waiting for transfers between devices, body(): lax.psum_scatter(jnp.dot(attn_rows, w_proj, preferred_element_type=jnp.fl...  97.9 us
    reduce_scatter x1, waiting for transfers between devices, body(): lax.psum_scatter(jnp.dot(hidden, w_second, preferred_element_type=jnp.flo...  96.6 us
    all_gather x1, waiting for transfers between devices, body(): lax.all_gather(grad_branch.astype(jnp.bfloat16), 'tp', axis=0, tiled=True)  80.8 us
    reduce_scatter x1, waiting for transfers between devices, body(): lax.psum_scatter(contract_cols(pre_low, w_first).astype(jnp.bfloat16), 't...  78.2 us
    all_gather x1, waiting for transfers between devices, body(): lax.all_gather(flat_tokens, 'tp', axis=0, tiled=True).astype(jnp.float32)  65.9 us
  transfers between devices with their start and end apart: 16, of which 12 were waited for; matrix products, arithmetic and copies ran while one was open for 23% of the time, Pallas kernels for 0%

commit v1 on v0

v1 whole, which is shorter than its diff:
```python
import functools
import math

import jax
import jax.numpy as jnp
from jax import lax
from jax.experimental import pallas as pl
from jax.experimental.pallas import tpu as pltpu
from jax.sharding import PartitionSpec as P

HD = 64
SEQ = 1370
Q_SPLIT = 2
LANES = 128
NEG = -1e30

norm_epsilon = 1e-06


def layer_norm_parts(values):
    center = values - jnp.mean(values, axis=-1, keepdims=True)
    spread = jnp.mean(center * center, axis=-1, keepdims=True)
    inverse = lax.rsqrt(spread + norm_epsilon)
    return center * inverse, inverse


def layer_norm_back(cotangent, xhat, inverse, norm_gain):
    scaled = cotangent * norm_gain
    first = jnp.mean(scaled, axis=-1, keepdims=True)
    second = jnp.mean(scaled * xhat, axis=-1, keepdims=True)
    return (
        inverse * (scaled - first - xhat * second),
        jnp.sum(cotangent * xhat, axis=tuple(range(cotangent.ndim - 1))),
        jnp.sum(cotangent, axis=tuple(range(cotangent.ndim - 1))),
    )


def dot(left, right, left_dim, right_dim):
    return lax.dot_general(
        left,
        right,
        (((left_dim,), (right_dim,)), ((), ())),
        preferred_element_type=jnp.float32,
    )


def head_operands(queries, keys, head):
    lane_q = lax.broadcasted_iota(jnp.int32, queries.shape, 1)
    lane_k = lax.broadcasted_iota(jnp.int32, keys.shape, 1)
    row_k = lax.broadcasted_iota(jnp.int32, keys.shape, 0)
    spare = (1 - head) * HD
    own_q = (lane_q >= head * HD) & (lane_q < (head + 1) * HD)
    scaled = queries.astype(jnp.float32) * 0.125
    query_plain = jnp.where(own_q, scaled, 0.0)
    query_mask = jnp.where(lane_q == spare, 1.0, query_plain)
    key_mask = jnp.where(
        lane_k == spare, jnp.where(row_k < SEQ, 0.0, NEG), keys.astype(jnp.float32)
    )
    return (
        query_plain.astype(jnp.bfloat16),
        query_mask.astype(jnp.bfloat16),
        key_mask.astype(jnp.bfloat16),
        own_q,
    )


def attend_kernel(q_ref, k_ref, v_ref, o_ref, lse_ref):
    queries, keys, values = q_ref[...], k_ref[...], v_ref[...]
    outs = []
    for head in range(2):
        _, query_mask, key_mask, own = head_operands(queries, keys, head)
        scores = dot(query_mask, key_mask, 1, 1)
        largest = jnp.max(scores, axis=-1, keepdims=True)
        expo = jnp.exp(scores - largest)
        totals = jnp.sum(expo, axis=-1, keepdims=True)
        outs.append(dot(expo.astype(jnp.bfloat16), values, 1, 0) / totals)
        logs = largest + jnp.log(totals)
        wide = jnp.transpose(jnp.broadcast_to(logs, (logs.shape[0], LANES)))
        lse_ref[pl.ds(head * 4, 4), :] = wide[:4]
    lane = lax.broadcasted_iota(jnp.int32, outs[0].shape, 1)
    o_ref[...] = jnp.where(lane < HD, outs[0], outs[1]).astype(o_ref.dtype)


def attend(joint, head_cols):
    seq_rows = joint.shape[0]
    pairs = head_cols // LANES
    block = seq_rows // Q_SPLIT
    cols = pl.BlockSpec((block, LANES), lambda p, i: (i, p))
    return pl.pallas_call(
        attend_kernel,
        name="attend",
        grid=(pairs, Q_SPLIT),
        in_specs=[
            cols,
            pl.BlockSpec((seq_rows, LANES), lambda p, i: (0, pairs + p)),
            pl.BlockSpec((seq_rows, LANES), lambda p, i: (0, 2 * pairs + p)),
        ],
        out_specs=[
            cols,
            pl.BlockSpec((None, None, 8, block), lambda p, i: (p, i, 0, 0)),
        ],
        out_shape=[
            jax.ShapeDtypeStruct((seq_rows, head_cols), jnp.bfloat16),
            jax.ShapeDtypeStruct((pairs, Q_SPLIT, 8, block), jnp.float32),
        ],
        compiler_params=pltpu.CompilerParams(vmem_limit_bytes=56 * 1024 * 1024),
        cost_estimate=pl.CostEstimate(
            flops=4 * seq_rows * seq_rows * head_cols * 4,
            bytes_accessed=8 * seq_rows * head_cols,
            transcendentals=seq_rows * seq_rows * head_cols // HD,
        ),
    )(joint, joint, joint)


def attend_back_kernel(
    q_ref, k_ref, v_ref, do_ref, lse_ref, dq_ref, dk_ref, dv_ref, qs_ref, vs_ref, dk_acc, dv_acc
):
    step = pl.program_id(1)

    @pl.when(step == 0)
    def _():
        dk_acc[...] = jnp.zeros_like(dk_acc)
        dv_acc[...] = jnp.zeros_like(dv_acc)
        qs_ref[...] = jnp.zeros_like(qs_ref)

    queries, keys, values, grads = q_ref[...], k_ref[...], v_ref[...], do_ref[...]
    parts = []
    for head in range(2):
        query_plain, query_mask, key_mask, own = head_operands(queries, keys, head)
        own_grads = jnp.where(own, grads.astype(jnp.float32), 0.0).astype(jnp.bfloat16)
        scores = dot(key_mask, query_mask, 1, 1)
        shares = jnp.exp(scores - lse_ref[head * 4 : head * 4 + 1, :])
        share_grad = dot(values, own_grads, 1, 1)
        inner = jnp.sum(shares * share_grad, axis=0, keepdims=True)
        score_grad = (shares * (share_grad - inner)).astype(jnp.bfloat16)
        dv_acc[...] += dot(shares.astype(jnp.bfloat16), own_grads, 1, 0)
        dk_acc[...] += dot(score_grad, query_plain, 1, 0)
        parts.append(dot(keys, score_grad, 0, 0))
    row = lax.broadcasted_iota(jnp.int32, parts[0].shape, 0)
    query_grad = jnp.transpose(jnp.where(row < HD, parts[0], parts[1])) * 0.125
    dq_ref[...] = query_grad.astype(dq_ref.dtype)
    qs_ref[...] += jnp.broadcast_to(jnp.sum(query_grad, axis=0, keepdims=True), qs_ref.shape)

    @pl.when(step == pl.num_programs(1) - 1)
    def _():
        dk_ref[...] = dk_acc[...].astype(dk_ref.dtype)
        dv_ref[...] = dv_acc[...].astype(dv_ref.dtype)
        vs_ref[...] = jnp.broadcast_to(
            jnp.sum(dv_acc[...], axis=0, keepdims=True), vs_ref.shape
        )


def attend_back(joint, grads, logs, head_cols):
    seq_rows = joint.shape[0]
    pairs = head_cols // LANES
    block = seq_rows // Q_SPLIT
    cols = pl.BlockSpec((block, LANES), lambda p, i: (i, p))
    whole = pl.BlockSpec((seq_rows, LANES), lambda p, i: (0, p))
    sums = pl.BlockSpec((8, LANES), lambda p, i: (0, p))
    return pl.pallas_call(
        attend_back_kernel,
        name="attend_back",
        grid=(pairs, Q_SPLIT),
        in_specs=[
            cols,
            pl.BlockSpec((seq_rows, LANES), lambda p, i: (0, pairs + p)),
            pl.BlockSpec((seq_rows, LANES), lambda p, i: (0, 2 * pairs + p)),
            cols,
            pl.BlockSpec((None, None, 8, block), lambda p, i: (p, i, 0, 0)),
        ],
        out_specs=[cols, whole, whole, sums, sums],
        out_shape=[jax.ShapeDtypeStruct((seq_rows, head_cols), jnp.bfloat16)] * 3
        + [jax.ShapeDtypeStruct((8, head_cols), jnp.float32)] * 2,
        scratch_shapes=[pltpu.VMEM((seq_rows, LANES), jnp.float32)] * 2,
        compiler_params=pltpu.CompilerParams(vmem_limit_bytes=56 * 1024 * 1024),
        cost_estimate=pl.CostEstimate(
            flops=10 * seq_rows * seq_rows * head_cols * 4,
            bytes_accessed=16 * seq_rows * head_cols,
            transcendentals=seq_rows * seq_rows * head_cols // HD,
        ),
    )(joint, joint, joint, grads, logs)


def body(
    tokens,
    w_query,
    w_key,
    w_value,
    w_out,
    w_up,
    w_down,
    norm1_gain,
    norm1_bias,
    query_bias,
    value_bias,
    out_bias,
    scale1,
    norm2_gain,
    norm2_bias,
    up_bias,
    down_bias,
    scale2,
    out_grad,
):
    image_count, shard_rows, width = tokens.shape
    tp_count = lax.axis_size("tp")
    tp_index = lax.axis_index("tp")
    local_rows = image_count * shard_rows
    head_cols = w_query.shape[1]
    hidden_cols = w_up.shape[1]
    hidden_all = hidden_cols * tp_count
    shard_width = w_up.shape[0]
    bf16 = jnp.bfloat16

    own_tokens = tokens.astype(jnp.float32)
    xhat1, inverse1 = layer_norm_parts(own_tokens)
    normed_own = (xhat1 * norm1_gain + norm1_bias).astype(bf16)
    w_joint = lax.all_gather(
        jnp.concatenate([w_query, w_key, w_value], axis=1), "fsdp", axis=0, tiled=True
    )
    normed = [
        lax.all_gather(normed_own[image], "tp", axis=0, tiled=True)
        for image in range(image_count)
    ]

    w_up_cols = lax.all_gather(w_up, "tp", axis=1, tiled=True)
    w_down_cols = lax.all_gather(w_down.T, "tp", axis=1, tiled=True)
    w_out_cols = lax.all_gather(w_out.T, "tp", axis=1, tiled=True)
    out_t = lax.all_gather(w_out_cols, "fsdp", axis=0, tiled=True)
    up = lax.all_gather(w_up_cols, "fsdp", axis=0, tiled=True)
    down_t = lax.all_gather(w_down_cols, "fsdp", axis=0, tiled=True)

    query_slice = lax.dynamic_slice_in_dim(query_bias, tp_index * head_cols, head_cols)
    value_slice = lax.dynamic_slice_in_dim(value_bias, tp_index * head_cols, head_cols)
    joint_bias = jnp.concatenate([query_slice, jnp.zeros((head_cols,), jnp.float32), value_slice])

    joints, logs, owned = [], [], []
    for image in range(image_count):
        joint = (dot(normed[image], w_joint, 1, 0) + joint_bias).astype(bf16)
        attended, log_totals = attend(joint, head_cols)
        joints.append(joint)
        logs.append(log_totals)
        owned.append(lax.all_to_all(attended, "tp", 0, 1, tiled=True))
    attended_own = jnp.concatenate(owned, axis=0)

    rows = own_tokens.reshape(local_rows, width)
    branch = dot(attended_own, out_t, 1, 1) + out_bias
    middle = rows + scale1 * branch
    xhat2, inverse2 = layer_norm_parts(middle)
    normed2 = (xhat2 * norm2_gain + norm2_bias).astype(bf16)
    preact = dot(normed2, up, 1, 0) + up_bias
    normal = 0.5 * (1.0 + lax.erf(preact * math.sqrt(0.5)))
    density = jnp.exp(-0.5 * preact * preact) * (1.0 / math.sqrt(2.0 * math.pi))
    hidden = (preact * normal).astype(bf16)
    slope = normal + preact * density
    feed = dot(hidden, down_t, 1, 1) + down_bias
    positions = tp_index * shard_rows + jnp.arange(shard_rows)
    row_valid = jnp.tile((positions < SEQ).astype(jnp.float32), image_count)[:, None]
    output = (row_valid * (middle + scale2 * feed)).astype(bf16).reshape(tokens.shape)

    grad_final = row_valid * out_grad.reshape(local_rows, width).astype(jnp.float32)
    scale2_part = jnp.sum(grad_final * feed, axis=0)
    grad_feed = scale2 * grad_final
    down_bias_part = jnp.sum(grad_feed, axis=0)
    feed_low = grad_feed.astype(bf16)
    down_grad = dot(feed_low, hidden, 0, 0).astype(bf16)
    down_grad = lax.psum_scatter(down_grad, "fsdp", scatter_dimension=0, tiled=True)
    pre_grad = dot(feed_low, down_t, 1, 0) * slope
    up_part = jnp.sum(pre_grad, axis=0)
    pre_low = pre_grad.astype(bf16)
    up_grad = dot(normed2, pre_low, 0, 0).astype(bf16)
    up_grad = lax.psum_scatter(up_grad, "fsdp", scatter_dimension=0, tiled=True)
    normed2_grad = dot(pre_low, up, 1, 1)
    middle_part, gain2_part, bias2_part = layer_norm_back(
        normed2_grad, xhat2, inverse2, norm2_gain
    )
    middle_grad = grad_final + middle_part
    scale1_part = jnp.sum(middle_grad * branch, axis=0)
    grad_branch = scale1 * middle_grad
    out_bias_part = jnp.sum(grad_branch, axis=0)
    branch_low = grad_branch.astype(bf16)
    attn_grad_own = dot(branch_low, out_t, 1, 0).astype(bf16)
    out_grad_t = dot(branch_low, attended_own, 0, 0).astype(bf16)
    out_grad_t = lax.psum_scatter(out_grad_t, "fsdp", scatter_dimension=0, tiled=True)

    joint_part = 0.0
    query_part = 0.0
    value_part = 0.0
    normed_grads = []
    for image in range(image_count):
        lower = image * shard_rows
        attn_grad = lax.all_to_all(
            attn_grad_own[lower : lower + shard_rows], "tp", 1, 0, tiled=True
        )
        dq, dk, dv, q_sums, v_sums = attend_back(joints[image], attn_grad, logs[image], head_cols)
        joint_low = jnp.concatenate([dq, dk, dv], axis=1)
        query_part = query_part + q_sums[0]
        value_part = value_part + v_sums[0]
        joint_part = joint_part + dot(normed[image], joint_low, 0, 0)
        partial = dot(joint_low, w_joint, 1, 1).astype(bf16)
        normed_grads.append(lax.psum_scatter(partial, "tp", scatter_dimension=0, tiled=True))
    joint_sum = lax.psum_scatter(
        joint_part.astype(bf16), "fsdp", scatter_dimension=0, tiled=True
    ).astype(jnp.float32)
    normed_grad = jnp.stack(normed_grads).astype(jnp.float32)
    input_part, gain1_part, bias1_part = layer_norm_back(normed_grad, xhat1, inverse1, norm1_gain)
    tokens_grad = middle_grad.reshape(tokens.shape) + input_part

    def own_columns(summed, count):
        return lax.psum_scatter(summed, "tp", scatter_dimension=1, tiled=True).astype(jnp.float32)

    w_up_grad = own_columns(up_grad, hidden_cols)
    w_down_grad = own_columns(down_grad, hidden_cols).T
    w_out_grad = own_columns(out_grad_t, head_cols).T

    def placed(part, like, count):
        return lax.dynamic_update_slice_in_dim(
            jnp.zeros_like(like), part, tp_index * count, 0
        )

    small = [
        gain1_part,
        bias1_part,
        placed(query_part, query_bias, head_cols),
        placed(value_part, value_bias, head_cols),
        out_bias_part,
        scale1_part,
        gain2_part,
        bias2_part,
        up_part,
        down_bias_part,
        scale2_part,
    ]
    sums = lax.psum(tuple(small), ("fsdp", "tp"))
    return (
        output,
        tokens_grad,
        joint_sum[:, :head_cols],
        joint_sum[:, head_cols : 2 * head_cols],
        joint_sum[:, 2 * head_cols :],
        w_out_grad,
        w_up_grad,
        w_down_grad,
        *sums,
    )


def solution(mesh):
    rows = P("fsdp", "tp", None)
    by_rows = P("fsdp", "tp")
    by_cols = P("tp", "fsdp")
    weights = (by_rows, by_rows, by_rows, by_cols, by_rows, by_cols)
    return jax.shard_map(
        body,
        mesh=mesh,
        in_specs=(rows, *weights, *([P()] * 11), rows),
        out_specs=(rows, rows, *weights, *([P()] * 11)),
        check_vma=False,
    )
```

time: 1560 us -> 862 us (0.55)
  waiting for transfers between devices: 851 us -> 510 us
  matrix products: 311 us -> 118 us
  other arithmetic: 155 us -> 20.4 us
  local copies, waits for them, and re-layouts: 126 us -> 24 us
  Pallas kernels: 0 us -> 89.3 us
  blocking collectives: 83.6 us -> 61.5 us
    reduce_scatter x8 -> x9, waiting for transfers between devices: 478 us -> 229 us  [the longest x2 111 us: body(): lax.psum_scatter(partial, 'tp', scatter_dimension=0, tiled=True)]
    dot_general x36 -> x15, matrix products: 311 us -> 118 us  [dot(): lax.dot_general(left, right, (((left_dim,), (right_dim,)), ((), ())), pre...]
    all_gather x6 -> x8, waiting for transfers between devices: 370 us -> 243 us  [the longest x2 107 us: body(): lax.all_gather(normed_own[image], 'tp', axis=0, tiled=True)]
    pallas_call x0 -> x4, Pallas kernels: none -> 89.3 us  [the longest x2 55.5 us: attend_back(): pl.pallas_call(attend_back_kernel, name='attend_back', grid=(pairs, Q_SPL...]
    convert_element_type x14 -> x3, other arithmetic: 68.3 us -> 3.87 us  [the longest x1 1.79 us: own_columns(): lax.psum_scatter(summed, 'tp', scatter_dimension=1, tiled=True)]
    reduce_sum x17 -> x6, other arithmetic: 58.4 us -> 7.97 us  [the longest x2 3.77 us: layer_norm_parts(): center = values - jnp.mean(values, axis=-1, keepdims=True)]
    reshape x5 -> x0, local copies, waits for them, and re-layouts: 40.2 us -> none  [the longest x1 14.4 us: body(): joint_grad.transpose(3, 0, 4, 1, 2, 5)]
    all_to_all x0 -> x4, waiting for transfers between devices: none -> 34 us  [the longest x2 17.8 us: body(): lax.all_to_all(attn_grad_own[lower:lower + shard_rows], 'tp', 1, 0, tiled...]
  transfers between devices with their start and end apart: 16 -> 21, of which waited for: 12 -> 15; matrix products, arithmetic and copies ran while one was open for 23% -> 13% of each run, Pallas kernels for 0% -> 10%
where the time goes in v1:
time: 862 us; the launch traced here: 855 us
  waiting for transfers between devices  510 us (59%)
  matrix products  118 us (14%)
  Pallas kernels  89.3 us (10%)
  blocking collectives  61.5 us (7%)
  local copies, waits for them, and re-layouts  24 us (3%)
  other arithmetic  20.4 us (2%)
  starting transfers between devices  17 us (2%)
  between operations  15 us (2%)
    dot_general x15, matrix products, dot(): lax.dot_general(left, right, (((left_dim,), (right_dim,)), ((), ())), pre...  118 us
    reduce_scatter x2, waiting for transfers between devices, body(): lax.psum_scatter(partial, 'tp', scatter_dimension=0, tiled=True)  111 us
    all_gather x2, waiting for transfers between devices, body(): lax.all_gather(normed_own[image], 'tp', axis=0, tiled=True)  107 us
    pallas_call x2, Pallas kernels, attend_back(): pl.pallas_call(attend_back_kernel, name='attend_back', grid=(pairs, Q_SPL...  55.5 us
    reduce_scatter x1, waiting for transfers between devices, body(): up_grad = lax.psum_scatter(up_grad, 'fsdp', scatter_dimension=0, tiled=True)  50.2 us
    all_gather x1, waiting for transfers between devices, body(): down_t = lax.all_gather(w_down_cols, 'fsdp', axis=0, tiled=True)  44.6 us
    psum x1, blocking collectives, body(): sums = lax.psum(tuple(small), ('fsdp', 'tp'))  42.9 us
    reduce_scatter x1, waiting for transfers between devices, body(): lax.psum_scatter(joint_part.astype(bf16), 'fsdp', scatter_dimension=0, ti...  40.6 us
  transfers between devices with their start and end apart: 21, of which 15 were waited for; matrix products, arithmetic and copies ran while one was open for 13% of the time, Pallas kernels for 10%

profile of v1, /device:TPU:0, one launch (start us, length us, event | category | flops | bytes accessed | tf_op | source)
XLA Modules:
  0.0 854.7 jit_solution(4728361107216698416)
XLA Ops:
  10.4 1.6 convert_reduce_fusion.1
  15.1 18.6 %all_gather.30 = bf16[128,1024]{0,1:T(8,128)(2,1)} all-gather(bf16[128,256]{0,1:T(8,128)(2,1)S(1)} %bitcast.94), channel_id=1, replica_groups=mesh['fsdp'=8,'tp'=4] {'tp'}, dimensions={1}, use_global_device_ids=true | all-gather | bytes 327680 | tf_op jit(solution)/shard_map/all_gather | solution.py:228
  33.8 9.3 %all-gather.15.cloned.1.call-done = bf16[128,4096]{1,0:T(8,128)(2,1)} async-done(((bf16[128,1024]{1,0:T(8,128)(2,1)}), bf16[128,4096]{1,0:T(8,128)(2,1)}) %all-gather.15.cloned.1.call-update) | async-done | bytes 1048592 | tf_op jit(solution)/shard_map/all_gather | solution.py:226
  43.1 29.7 %all-gather.19.cloned.1.call-done = bf16[128,4096]{0,1:T(8,128)(2,1)} async-done(((bf16[128,1024]{0,1:T(8,128)(2,1)}), bf16[128,4096]{0,1:T(8,128)(2,1)}) %all-gather.19.cloned.1.call-update) | async-done | bytes 1048592 | tf_op jit(solution)/shard_map/all_gather | solution.py:227
  74.4 25.9 %all-gather.11.cloned.1.call-done = bf16[1024,768]{1,0:T(8,128)(2,1)} async-done(((bf16[128,768]{1,0:T(8,128)(2,1)}), bf16[1024,768]{1,0:T(8,128)(2,1)}) %all-gather.11.cloned.1.call-update) | async-done | bytes 1572880 | tf_op jit(solution)/shard_map/all_gather | solution.py:218
  100.2 60.1 %all-gather.23.cloned.1.call-done = bf16[1,1376,1024]{2,1,0:T(8,128)(2,1)} async-done(((bf16[1,344,1024]{2,1,0:T(8,128)(2,1)}), bf16[1,1376,1024]{2,1,0:T(8,128)(2,1)}) %all-gather.23.cloned.1.call-update) | async-done | bytes 2818064 | tf_op jit(solution)/shard_map/all_gather | solution.py:222
  160.3 5.9 add_convert_fusion.1.q_ref.k_ref.v_ref
  166.2 16.9 %attend.2 = (bf16[1376,256]{1,0:T(8,128)(2,1)}, f32[2,2,8,688]{3,2,1,0:T(8,128)}) custom-call(bf16[1376,768]{1,0:T(8,128)(2,1)} %add_convert_fusion.1.q_ref.k_ref.v_ref, bf16[1376,768]{1,0:T(8,128)(2,1)} %add_convert_fusion.1.q_ref.k_ref.v_ref, bf16[1376,768]{1,0:T(8,128)(2,1)} %add_convert_fusion.1.q_ref.k_ref.v_ref), custom_call_target="tpu_custom_call" | custom-call | flops 7755268096 | bytes 2818048 | tf_op jit(solution)/shard_map/attend/pallas_call | solution.py:89
  183.1 3.7 all-to-all-start
  186.8 47.1 %all-gather.25.cloned.1.call-done = bf16[1,1376,1024]{2,1,0:T(8,128)(2,1)} async-done(((bf16[1,344,1024]{2,1,0:T(8,128)(2,1)}), bf16[1,1376,1024]{2,1,0:T(8,128)(2,1)}) %all-gather.25.cloned.1.call-update) | async-done | bytes 2818064 | tf_op jit(solution)/shard_map/all_gather | solution.py:222
  233.9 6.0 add_convert_fusion.q_ref.k_ref.v_ref
  239.9 17.0 %attend.3 = (bf16[1376,256]{1,0:T(8,128)(2,1)}, f32[2,2,8,688]{3,2,1,0:T(8,128)}) custom-call(bf16[1376,768]{1,0:T(8,128)(2,1)} %add_convert_fusion.q_ref.k_ref.v_ref, bf16[1376,768]{1,0:T(8,128)(2,1)} %add_convert_fusion.q_ref.k_ref.v_ref, bf16[1376,768]{1,0:T(8,128)(2,1)} %add_convert_fusion.q_ref.k_ref.v_ref), custom_call_target="tpu_custom_call" | custom-call | flops 7755268096 | bytes 2818048 | tf_op jit(solution)/shard_map/attend/pallas_call | solution.py:89
  256.9 4.2 all-to-all-start.1
  263.4 16.2 %all-to-all-done.1 = bf16[4,344,256]{2,1,0:T(8,128)(2,1)} async-done(((bf16[4,344,256]{2,1,0:T(8,128)(2,1)}), bf16[4,344,256]{2,1,0:T(8,128)(2,1)}, u32[]{:S(2)}, u32[]{:S(2)}) %all-to-all-start.1) | async-done | bytes 704544 | tf_op jit(solution)/shard_map/all_to_all | solution.py:243
  282.6 6.2 multiply_add_fusion.1
  288.8 2.2 reduce_sum.155
  291.9 26.7 %all-gather.17.cloned.1.call-done = bf16[1024,4096]{1,0:T(8,128)(2,1)} async-done(((bf16[128,4096]{1,0:T(8,128)(2,1)}), bf16[1024,4096]{1,0:T(8,128)(2,1)}) %all-gather.17.cloned.1.call-update) | async-done | bytes 8388624 | tf_op jit(solution)/shard_map/all_gather | solution.py:230
  318.5 13.1 %multiply_convert_fusion = (bf16[688,4096]{1,0:T(8,128)(2,1)}, f32[688,4096]{1,0:T(8,128)}) fusion(f32[4096]{0:T(1024)S(1)} %copy-done.31, bf16[1024,4096]{1,0:T(8,128)(2,1)} %all-gather.17.cloned.1.call-done, f32[688,1024]{1,0:T(8,128)S(1)} %copy-done.2, f32[1024]{0:T(1024)S(1)} %copy-done.35, f32[1024]{0:T(1024)S(1)} %copy-done.34, ...), kind=kOutput, calls=%fused_computation.6 | convolution fusion | flops 5791793152 | bytes 28145024 | tf_op jit(solution)/shard_map/dot_general | solution.py:39
  331.6 44.6 %all-gather.21.cloned.1.call-done = bf16[1024,4096]{0,1:T(8,128)(2,1)} async-done(((bf16[128,4096]{0,1:T(8,128)(2,1)}), bf16[1024,4096]{0,1:T(8,128)(2,1)}) %all-gather.21.cloned.1.call-update) | async-done | bytes 8388624 | tf_op jit(solution)/shard_map/all_gather | solution.py:231
  376.3 15.5 %fusion.29 = (f32[4096]{0:T(1024)S(1)}, bf16[688,4096]{1,0:T(8,128)(2,1)}) fusion(f32[688,4096]{1,0:T(8,128)} %get-tuple-element.141, f32[4096]{0:T(1024)S(1)} %copy-done.31, bf16[688,1024]{1,0:T(8,128)(2,1)} %multiply_convert_fusion.1, bf16[1024,4096]{0,1:T(8,128)(2,1)} %all-gather.21.cloned.1.call-done), kind=kOutput, calls=%fused_computation.88 | convolution fusion | flops 5805174784 | bytes 26738688 | tf_op jit(solution)/shard_map/dot_general | solution.py:39
  391.8 11.1 %multiply_reduce_fusion.2 = (f32[1024]{0:T(1024)S(1)}, f32[688]{0:T(1024)S(1)}, f32[688]{0:T(1024)S(1)}, f32[1024]{0:T(1024)S(1)}, f32[688,1024]{1,0:T(8,128)S(1)}) fusion(f32[688,1024]{1,0:T(8,128)S(1)} %copy-done.2, f32[688]{0:T(1024)S(1)} %add_rsqrt_fusion, f32[688]{0:T(1024)S(1)} %broadcast_multiply_fusion.2, f32[1024]{0:T(1024)S(1)} %copy-done.34, ...), kind=kOutput, calls=%fused_computation.35 | convolution fusion | flops 5777699840 | bytes 19684096 | tf_op jit(solution)/shard_map/dot_general | solution.py:39
  403.0 11.0 %multiply_reduce_fusion = (f32[1024]{0:T(1024)S(1)}, bf16[688,1024]{1,0:T(8,128)(2,1)}, f32[1024]{0:T(1024)S(1)}, f32[1024]{0:T(1024)S(1)}, f32[688,1024]{1,0:T(8,128)S(1)}) fusion(bf16[2,344,1024]{2,1,0:T(8,128)(2,1)S(1)} %copy-done.4, f32[1024]{0:T(1024)S(1)} %copy-done.32, f32[688]{0:T(1024)S(1)} %mul.196, f32[688,1024]{1,0:T(8,128)S(1)} %copy-done.2, ...), kind=kOutput, calls=%fused_computation.33 | convolution fusion | flops 5786858496 | bytes 28161472 | tf_op jit(solution)/shard_map/dot_general | solution.py:39
  415.6 4.6 convolution_convert_fusion.4
  420.2 11.2 %convolution_convert_fusion = bf16[1024,4096]{1,0:T(8,128)(2,1)} fusion(bf16[688,1024]{1,0:T(8,128)(2,1)} %multiply_convert_fusion.1, bf16[688,4096]{1,0:T(8,128)(2,1)} %get-tuple-element.140), kind=kOutput, calls=%fused_computation.8 | convolution fusion | flops 5775556608 | bytes 15433728 | tf_op jit(solution)/shard_map/dot_general | solution.py:39
  431.5 12.1 %convolution_convert_fusion.1 = bf16[1024,4096]{1,0:T(8,128)(2,1)} fusion(bf16[688,4096]{1,0:T(8,128)(2,1)} %get-tuple-element.144, f32[688,1024]{1,0:T(8,128)S(1)} %copy-done.2, f32[1024]{0:T(1024)S(1)} %copy-done.35, f32[1024]{0:T(1024)S(1)} %copy-done.34, f32[688]{0:T(1024)S(1)} %add_rsqrt_fusion, f32[688]{0:T(1024)S(1)} %broadcast_multiply_fusion.2), kind=kOutput, calls=%fused_computation.9 | convolution fusion | flops 5779079168 | bytes 16856448 | tf_op jit(solution)/shard_map/dot_general | solution.py:39
  443.6 1.8 copy-done.7
  445.3 3.3 convolution_convert_fusion.5
  449.7 4.6 all-to-all-start.3
  455.2 17.8 %all-to-all-done.3 = bf16[344,4,256]{2,0,1:T(8,128)(2,1)S(1)} async-done(((bf16[344,4,256]{2,0,1:T(8,128)(2,1)}), bf16[344,4,256]{2,0,1:T(8,128)(2,1)S(1)}, u32[]{:S(2)}, u32[]{:S(2)}) %all-to-all-start.3) | async-done | bytes 704544 | tf_op jit(solution)/shard_map/all_to_all | solution.py:292
  473.0 3.5 all-to-all-start.2
  476.6 27.7 %attend_back.3 = (bf16[1376,256]{1,0:T(8,128)(2,1)}, bf16[1376,256]{1,0:T(8,128)(2,1)}, bf16[1376,256]{1,0:T(8,128)(2,1)}, f32[8,256]{1,0:T(8,128)}, f32[8,256]{1,0:T(8,128)}) custom-call(bf16[1376,768]{1,0:T(8,128)(2,1)} %add_convert_fusion.q_ref.k_ref.v_ref, bf16[1376,768]{1,0:T(8,128)(2,1)} %add_convert_fusion.q_ref.k_ref.v_ref, ...), custom_call_target="tpu_custom_call" | custom-call | flops 19388170240 | bytes 5636096 | tf_op jit(solution)/shard_map/attend_back/pallas_call | solution.py:160
  506.4 27.7 %attend_back.2 = (bf16[1376,256]{1,0:T(8,128)(2,1)}, bf16[1376,256]{1,0:T(8,128)(2,1)}, bf16[1376,256]{1,0:T(8,128)(2,1)}, f32[8,256]{1,0:T(8,128)}, f32[8,256]{1,0:T(8,128)}) custom-call(bf16[1376,768]{1,0:T(8,128)(2,1)} %add_convert_fusion.1.q_ref.k_ref.v_ref, bf16[1376,768]{1,0:T(8,128)(2,1)} %add_convert_fusion.1.q_ref.k_ref.v_ref, ...), custom_call_target="tpu_custom_call" | custom-call | flops 19388170240 | bytes 5636096 | tf_op jit(solution)/shard_map/attend_back/pallas_call | solution.py:160
  537.5 2.8 fusion.13
  540.3 3.9 add_convert_fusion.2
  545.3 5.4 convolution_convert_fusion.2
  550.7 2.0 copy-done.17
  552.7 5.7 convolution_convert_fusion.3
  561.1 50.2 %reduce-scatter.20.cloned.1.call-done = bf16[128,4096]{1,0:T(8,128)(2,1)} async-done(((bf16[1024,4096]{1,0:T(8,128)(2,1)}), bf16[128,4096]{1,0:T(8,128)(2,1)}) %reduce-scatter.20.cloned.1.call-update) | async-done | bytes 1048592 | tf_op jit(solution)/shard_map/reduce_scatter | solution.py:272
  612.2 40.6 %reduce-scatter.14.cloned.1.call-done = bf16[128,768]{1,0:T(8,128)(2,1)} async-done(((bf16[1024,768]{1,0:T(8,128)(2,1)}), bf16[128,768]{1,0:T(8,128)(2,1)}) %reduce-scatter.14.cloned.1.call-update) | async-done | bytes 196624 | tf_op jit(solution)/shard_map/reduce_scatter | solution.py:302
  652.8 1.7 fusion.28
  654.4 20.6 %reduce-scatter.18.cloned.1.call-done = bf16[128,256]{1,0:T(8,128)(2,1)} async-done(((bf16[128,1024]{1,0:T(8,128)(2,1)}), bf16[128,256]{1,0:T(8,128)(2,1)}) %reduce-scatter.18.cloned.1.call-update) | async-done | bytes 65552 | tf_op jit(solution)/shard_map/reduce_scatter | solution.py:310
  676.7 54.2 %reduce-scatter.12.cloned.1.call-done = bf16[344,1024]{1,0:T(8,128)(2,1)} async-done(((bf16[1376,1024]{1,0:T(8,128)(2,1)}), bf16[344,1024]{1,0:T(8,128)(2,1)}) %reduce-scatter.12.cloned.1.call-update) | async-done | bytes 704528 | tf_op jit(solution)/shard_map/reduce_scatter | solution.py:301
  730.9 57.2 %reduce-scatter.10.cloned.1.call-done = bf16[344,1024]{1,0:T(8,128)(2,1)} async-done(((bf16[1376,1024]{1,0:T(8,128)(2,1)}), bf16[344,1024]{1,0:T(8,128)(2,1)}) %reduce-scatter.10.cloned.1.call-update) | async-done | bytes 704528 | tf_op jit(solution)/shard_map/reduce_scatter | solution.py:301
  788.1 2.8 fusion.12
  790.9 42.9 %all-reduce = (f32[1024]{0:T(1024)}, f32[1024]{0:T(1024)}, f32[1024]{0:T(1024)}, f32[1024]{0:T(1024)}, f32[1024]{0:T(1024)}, /*index=5*/f32[1024]{0:T(1024)}, f3...) all-reduce(f32[1024]{0:T(1024)S(1)} %get-tuple-element.106, ...), channel_id=1, replica_groups=mesh['fsdp'=8,'tp'=4] {'fsdp','tp'}, use_global_device_ids=true, to_apply=%region_18.0 | all-reduce | flops 14336 | bytes 114688 | tf_op jit(solution)/shard_map/psum | solution.py:334
  833.8 3.6 fusion.10
  839.4 6.5 reduce-scatter.22.cloned.1.call-done
  845.9 1.8 convert_element_type.99
  (163 shorter events, 31.2 us)
Async XLA Ops:
  7.2 4.9 copy-start
  7.2 5.4 copy-start.28
  7.2 5.4 copy-start.23
  7.2 35.8 %all-gather.15.cloned.1.call-start = ((), (), s32[]{:S(2)}) async-start(), calls=%async_computation.15 | async-start | bytes 1310720 | tf_op jit(solution)/shard_map/all_gather | solution.py:226
  8.0 64.8 %all-gather.19.cloned.1.call-start = ((), (), s32[]{:S(2)}) async-start(), calls=%async_computation.17 | async-start | bytes 1310720 | tf_op jit(solution)/shard_map/all_gather | solution.py:227
  8.7 91.5 %all-gather.11.cloned.1.call-start = ((), (), s32[]{:S(2)}) async-start(), calls=%async_computation.13 | async-start | bytes 1769472 | tf_op jit(solution)/shard_map/all_gather | solution.py:218
  10.4 149.9 %all-gather.23.cloned.1.call-start = ((), (), s32[]{:S(2)}) async-start(), calls=%async_computation.28 | async-start | bytes 3522560 | tf_op jit(solution)/shard_map/all_gather | solution.py:222
  12.1 2.4 copy-start.18
  14.4 219.5 %all-gather.25.cloned.1.call-start = ((), (), s32[]{:S(2)}) async-start(), calls=%async_computation.29 | async-start | bytes 3522560 | tf_op jit(solution)/shard_map/all_gather | solution.py:222
  15.0 267.6 %all-gather.13.cloned.1.call-start = ((), (), s32[]{:S(2)}) async-start(), calls=%async_computation.14 | async-start | bytes 2359296 | tf_op jit(solution)/shard_map/all_gather | solution.py:229
  33.7 284.8 %all-gather.17.cloned.1.call-start = ((), (), s32[]{:S(2)}) async-start(), calls=%async_computation.16 | async-start | bytes 9437184 | tf_op jit(solution)/shard_map/all_gather | solution.py:230
  43.0 333.2 %all-gather.21.cloned.1.call-start = ((), (), s32[]{:S(2)}) async-start(), calls=%async_computation.18 | async-start | bytes 9437184 | tf_op jit(solution)/shard_map/all_gather | solution.py:231
  183.1 73.7 %all-to-all-start = ((bf16[4,344,256]{2,1,0:T(8,128)(2,1)}), bf16[4,344,256]{2,1,0:T(8,128)(2,1)S(1)}, u32[]{:S(2)}, u32[]{:S(2)}) async-start(bf16[4,344,256]{2,1,0:T(8,128)(2,1)} %bitcast.92), calls=%async_computation | async-start | bytes 1409024 | tf_op jit(solution)/shard_map/all_to_all | solution.py:243
  239.9 21.9 %copy-start.3 = (bf16[2,344,1024]{2,1,0:T(8,128)(2,1)S(1)}, bf16[2,344,1024]{2,1,0:T(8,128)(2,1)}, u32[]{:S(2)}) copy-start(bf16[2,344,1024]{2,1,0:T(8,128)(2,1)} %param.37) | copy-start | bytes 4227076
  239.9 21.9 %copy-start.27 = (f32[1024]{0:T(1024)S(1)}, f32[1024]{0:T(1024)}, u32[]{:S(2)}) copy-start(f32[1024]{0:T(1024)} %param.36) | copy-start | bytes 12292
  256.9 22.7 %all-to-all-start.1 = ((bf16[4,344,256]{2,1,0:T(8,128)(2,1)}), bf16[4,344,256]{2,1,0:T(8,128)(2,1)}, u32[]{:S(2)}, u32[]{:S(2)}) async-start(bf16[4,344,256]{2,1,0:T(8,128)(2,1)} %bitcast.91), calls=%async_computation.1 | async-start | bytes 1409024 | tf_op jit(solution)/shard_map/all_to_all | solution.py:243
  261.1 283.2 %reduce-scatter.16.cloned.1.call-start = ((), (), s32[]{:S(2)}) async-start(), calls=%async_computation.22 | async-start | bytes 2359296 | tf_op jit(solution)/shard_map/reduce_scatter | solution.py:284
  263.3 19.3 %copy-start.33 = (f32[1024]{0:T(1024)S(1)}, f32[1024]{0:T(1024)}, u32[]{:S(2)}) copy-start(f32[1024]{0:T(1024)} %param.30) | copy-start | bytes 12292
  263.3 19.3 %copy-start.36 = (f32[1024]{0:T(1024)S(1)}, f32[1024]{0:T(1024)}, u32[]{:S(2)}) copy-start(f32[1024]{0:T(1024)} %param.31) | copy-start | bytes 12292
  288.8 2.6 copy-start.2
  288.8 29.7 %copy-start.31 = (f32[4096]{0:T(1024)S(1)}, f32[4096]{0:T(1024)}, u32[]{:S(2)}) copy-start(f32[4096]{0:T(1024)} %param.34) | copy-start | bytes 49156
  288.8 29.7 %copy-start.34 = (f32[1024]{0:T(1024)S(1)}, f32[1024]{0:T(1024)}, u32[]{:S(2)}) copy-start(f32[1024]{0:T(1024)} %param.32) | copy-start | bytes 12292
  288.8 29.7 %copy-start.35 = (f32[1024]{0:T(1024)S(1)}, f32[1024]{0:T(1024)}, u32[]{:S(2)}) copy-start(f32[1024]{0:T(1024)} %param.33) | copy-start | bytes 12292
  376.3 26.7 %slice-start = ((s8[8388608]{0:T(1024)(128)(4,1)}), s8[4194304]{0:T(1024)(128)(4,1)S(1)}, s32[]{:S(2)}) async-start(s8[8388608]{0:T(1024)(128)(4,1)} %bitcast.97), calls=%async_computation.30 | async-start | bytes 8388608
  391.8 11.2 %copy-start.4 = (bf16[2,344,1024]{2,1,0:T(8,128)(2,1)S(1)}, bf16[2,344,1024]{2,1,0:T(8,128)(2,1)}, u32[]{:S(2)}) copy-start(bf16[2,344,1024]{2,1,0:T(8,128)(2,1)} %param.37) | copy-start | bytes 4227076
  391.8 11.2 %slice-start.1 = ((s8[8388608]{0:T(1024)(128)(4,1)}), s8[4194304]{0:T(1024)(128)(4,1)S(1)}, s32[]{:S(2)}) async-start(s8[8388608]{0:T(1024)(128)(4,1)} %bitcast.97), calls=%async_computation.31 | async-start | bytes 8388608
  391.8 11.2 %copy-start.32 = (f32[1024]{0:T(1024)S(1)}, f32[1024]{0:T(1024)}, u32[]{:S(2)}) copy-start(f32[1024]{0:T(1024)} %param.35) | copy-start | bytes 12292
  391.8 11.2 %copy-start.37 = (f32[688,1024]{1,0:T(8,128)S(1)}, f32[688,1024]{1,0:T(8,128)}, u32[]{:S(2)}) copy-start(f32[688,1024]{1,0:T(8,128)} %get-tuple-element.139) | copy-start | bytes 8454148
  420.2 138.3 %reduce-scatter.24.cloned.1.call-start = ((), (), s32[]{:S(2)}) async-start(), calls=%async_computation.26 | async-start | bytes 9437184 | tf_op jit(solution)/shard_map/reduce_scatter | solution.py:267
  431.4 179.9 %reduce-scatter.20.cloned.1.call-start = ((), (), s32[]{:S(2)}) async-start(), calls=%async_computation.24 | async-start | bytes 9437184 | tf_op jit(solution)/shard_map/reduce_scatter | solution.py:272
  449.7 23.4 %all-to-all-start.3 = ((bf16[344,4,256]{2,0,1:T(8,128)(2,1)}), bf16[344,4,256]{2,0,1:T(8,128)(2,1)S(1)}, u32[]{:S(2)}, u32[]{:S(2)}) async-start(bf16[344,4,256]{2,0,1:T(8,128)(2,1)} %bitcast.77), calls=%async_computation.4 | async-start | bytes 1409024 | tf_op jit(solution)/shard_map/all_to_all | solution.py:292
  473.0 3.6 copy-start.12
  473.0 32.5 %all-to-all-start.2 = ((bf16[344,4,256]{2,0,1:T(8,128)(2,1)}), bf16[344,4,256]{2,0,1:T(8,128)(2,1)S(1)}, u32[]{:S(2)}, u32[]{:S(2)}) async-start(bf16[344,4,256]{2,0,1:T(8,128)(2,1)} %bitcast.78), calls=%async_computation.2 | async-start | bytes 1409024 | tf_op jit(solution)/shard_map/all_to_all | solution.py:292
  476.6 176.2 %reduce-scatter.14.cloned.1.call-start = ((), (), s32[]{:S(2)}) async-start(), calls=%async_computation.21 | async-start | bytes 1769472 | tf_op jit(solution)/shard_map/reduce_scatter | solution.py:302
  506.4 29.1 %copy-start.13 = (bf16[1376,256]{1,0:T(8,128)(2,1)S(1)}, bf16[1376,256]{1,0:T(8,128)(2,1)}, u32[]{:S(2)}) copy-start(bf16[1376,256]{1,0:T(8,128)(2,1)} %get-tuple-element.41) | copy-start | bytes 2113540
  537.5 2.8 copy-start.16
  537.5 2.8 copy-start.29
  544.2 130.9 %reduce-scatter.18.cloned.1.call-start = ((), (), s32[]{:S(2)}) async-start(), calls=%async_computation.23 | async-start | bytes 327680 | tf_op jit(solution)/shard_map/reduce_scatter | solution.py:310
  545.0 185.9 %reduce-scatter.12.cloned.1.call-start = ((), (), s32[]{:S(2)}) async-start(), calls=%async_computation.20 | async-start | bytes 3522560 | tf_op jit(solution)/shard_map/reduce_scatter | solution.py:301
  550.7 237.4 %reduce-scatter.10.cloned.1.call-start = ((), (), s32[]{:S(2)}) async-start(), calls=%async_computation.19 | async-start | bytes 3522560 | tf_op jit(solution)/shard_map/reduce_scatter | solution.py:301
  558.4 229.7 %copy-start.1 = (bf16[2,344,1024]{2,1,0:T(8,128)(2,1)S(1)}, bf16[2,344,1024]{2,1,0:T(8,128)(2,1)}, u32[]{:S(2)}) copy-start(bf16[2,344,1024]{2,1,0:T(8,128)(2,1)} %param.19) | copy-start | bytes 4227076
  558.4 229.7 %copy-start.19 = (f32[2,344]{1,0:T(2,128)S(1)}, f32[2,344]{1,0:T(2,128)}, u32[]{:S(2)}) copy-start(f32[2,344]{1,0:T(2,128)} %copy-done.18) | copy-start | bytes 8260
  558.4 229.7 %copy-start.22 = (f32[2,344]{1,0:T(2,128)S(1)}, f32[2,344]{1,0:T(2,128)}, u32[]{:S(2)}) copy-start(f32[2,344]{1,0:T(2,128)} %copy-done.21) | copy-start | bytes 8260
  558.4 229.7 %copy-start.24 = (f32[1024]{0:T(1024)S(1)}, f32[1024]{0:T(1024)}, u32[]{:S(2)}) copy-start(f32[1024]{0:T(1024)} %param.26) | copy-start | bytes 12292
  558.4 279.0 %reduce-scatter.26.cloned.1.call-start = ((), (), s32[]{:S(2)}) async-start(), calls=%async_computation.27 | async-start | bytes 1310720 | tf_op jit(solution)/shard_map/reduce_scatter | solution.py:310
  559.0 286.9 %reduce-scatter.22.cloned.1.call-start = ((), (), s32[]{:S(2)}) async-start(), calls=%async_computation.25 | async-start | bytes 1310720 | tf_op jit(solution)/shard_map/reduce_scatter | solution.py:310
  730.9 103.0 %copy-start.8 = (bf16[344,1024]{1,0:T(8,128)(2,1)S(1)}, bf16[344,1024]{1,0:T(8,128)(2,1)}, u32[]{:S(2)}) copy-start(bf16[344,1024]{1,0:T(8,128)(2,1)} %reduce-scatter.12.cloned.1.call-done) | copy-start | bytes 2113540
  788.1 45.8 %copy-start.9 = (bf16[344,1024]{1,0:T(8,128)(2,1)S(1)}, bf16[344,1024]{1,0:T(8,128)(2,1)}, u32[]{:S(2)}) copy-start(bf16[344,1024]{1,0:T(8,128)(2,1)} %reduce-scatter.10.cloned.1.call-done) | copy-start | bytes 2113540
  (13 other events, 19.8 us)
Sparse Core Ops, SparseCore 0:
  9.6 33.3 all-gather.14
  44.6 28.1 all-gather.18
  75.3 24.9 all-gather.10
  102.2 58.0 all-gather.22
  162.3 71.5 all-gather.24
  235.6 26.6 all-gather.12
  264.2 54.2 all-gather.16
  320.4 55.8 all-gather.20
  420.3 41.1 reduce-scatter.15
  464.7 71.4 reduce-scatter.23
  539.7 71.4 reduce-scatter.19
  614.4 38.3 reduce-scatter.13
  655.0 19.9 reduce-scatter.17
  677.3 53.5 reduce-scatter.11
  733.0 54.9 reduce-scatter.9
  790.2 27.6 reduce-scatter.25
  820.1 25.7 reduce-scatter.21
